TPU v7x, 32 devices: a whole 2x2x4 slice. The times are simulated.
32 devices in a mesh: ctx: 8 (over z, y), grp: 4 (over x, core).
Axes of the slice: x: 2, y: 2, z: 4, core: 2. Of those that a mesh axis runs over, the one named last changes fastest.
Arguments:
- tokens: bfloat16 [4, 512, 8192], P('grp', 'ctx'), may hold values from -6 to 6
- queries: bfloat16 [4, 512, 4096], P('grp', 'ctx'), may hold values from -32 to 32
- key_value_weight: bfloat16 [8192, 1024], P('grp'), may hold values from -0.0625 to 0.0625
- adapter_down_weight: bfloat16 [8192, 128], P('grp'), may hold values from -0.0625 to 0.0625
- adapter_up_weight: bfloat16 [2, 64, 512], replicated, may hold values from -0.75 to 0.75
- tile_request_mask: int32 [4, 4, 4], P('grp'), may hold values 0 or 1
- lengths: int32 [4], P('grp'), may hold values from 128 to 512, as said below
- page_lookup_table: int32 [4, 128], P(None, 'ctx'), may hold values from 0 to 63, as said below
Outputs:
- attended: bfloat16 [4, 512, 4096], P('grp', 'ctx')
- decode_cache: bfloat16 [4, 128, 4, 1024], P('grp', 'ctx')
Inputs may be any that keep to these rules, and one draw needn't show every extreme that they name: `page_lookup_table`: pages of positions held by one index of ctx go to decode-cache rows of that same index. Every decode group receives exactly 16 pages into distinct slots from the pages of each index of ctx. From the pages of one rollout on one index of ctx, at most max(2, ceil(4)) go to one group, and exactly that many to some group. `lengths`: some rollout has all 512 positions live.
All inputs are finite; a program needn't handle non-finite values. No bound on the sum of `tile_request_mask` on one device may be relied on, other than what follows from the above.
Results may differ from a plain program's by a relative error of at most 0.028.
Values may be sent and summed in bfloat16 or wider, within the bound.
A program may use at most 64 MiB of HBM per device.

v0:
```python
import jax
import jax.numpy as jnp
from jax import lax
from jax.sharding import PartitionSpec as P

HEAD_SIZE = 128
HQ = 32
KEY_VALUE_HEADS = 4
PAGE = 4
TILE = 128
THETA = 500000.0
ADAPTER_SCALE = 0.5


def rotate(key_rows, token_positions):
    half_split = HEAD_SIZE // 2
    freq = THETA ** (-(2.0 * jnp.arange(half_split, dtype=jnp.float32)) / HEAD_SIZE)
    angle = token_positions.astype(jnp.float32)[:, None] * freq[None, :]
    cosine = jnp.cos(angle)[:, None, :]
    sine = jnp.sin(angle)[:, None, :]
    first = key_rows[..., :half_split]
    second = key_rows[..., half_split:]
    return jnp.concatenate([first * cosine - second * sine, second * cosine + first * sine], -1)


def send_pages(own, page_lookup_table, groups):
    column_width = own.shape[1]
    ppd = own.shape[0] // PAGE
    most = max(2, -(-ppd // groups))
    me = lax.axis_index("grp")
    dest = page_lookup_table // ppd
    slot = page_lookup_table % ppd
    earlier = jnp.arange(ppd)[:, None] > jnp.arange(ppd)[None, :]
    same = dest[:, :, None] == dest[:, None, :]
    order = jnp.sum(same & earlier[None], axis=2)
    my_dest = lax.dynamic_index_in_dim(dest, me, 0, keepdims=False)
    my_order = lax.dynamic_index_in_dim(order, me, 0, keepdims=False)
    pick = (my_dest[None, None, :] == jnp.arange(groups)[:, None, None]) & (
        my_order[None, None, :] == jnp.arange(most)[None, :, None]
    )
    pages = own.reshape(ppd, PAGE * column_width)
    outgoing = jnp.einsum(
        "gck,kf->gcf", pick.astype(jnp.bfloat16), pages, preferred_element_type=jnp.float32
    ).astype(jnp.bfloat16)
    incoming = lax.all_to_all(outgoing, "grp", split_axis=0, concat_axis=0, tiled=True)
    place = (
        (dest[None, :, None, :] == me)
        & (order[None, :, None, :] == jnp.arange(most)[None, None, :, None])
        & (slot[None, :, None, :] == jnp.arange(ppd)[:, None, None, None])
    )
    place = jnp.any(place, axis=3).reshape(ppd, groups * most)
    cache = jnp.dot(
        place.astype(jnp.bfloat16),
        incoming.reshape(groups * most, PAGE * column_width),
        preferred_element_type=jnp.float32,
    )
    return cache.astype(jnp.bfloat16).reshape(1, ppd, PAGE, column_width)


def local(
    tokens,
    queries,
    key_value_weight,
    adapter_down_weight,
    adapter_up_weight,
    tile_request_mask,
    lengths,
    page_lookup_table,
):
    groups = lax.axis_size("grp")
    tok = tokens.shape[1]
    column_width = key_value_weight.shape[1]
    half_split = column_width // 2
    rank_count = adapter_up_weight.shape[1]
    group = HQ // KEY_VALUE_HEADS
    ctx_pos = lax.axis_index("ctx")
    token_positions = ctx_pos * tok + jnp.arange(tok, dtype=jnp.int32)
    mixed_output = lax.all_to_all(tokens[0], "grp", split_axis=1, concat_axis=0, tiled=True)
    summed_output = lax.psum_scatter(
        jnp.concatenate(
            [
                jnp.dot(mixed_output, key_value_weight, preferred_element_type=jnp.float32),
                jnp.dot(mixed_output, adapter_down_weight, preferred_element_type=jnp.float32),
            ],
            1,
        ).astype(jnp.bfloat16),
        "grp",
        scatter_dimension=0,
        tiled=True,
    ).astype(jnp.float32)
    low_rank_state = summed_output[:, column_width:].astype(jnp.bfloat16)
    key_rows = summed_output[:, :half_split] + ADAPTER_SCALE * jnp.dot(
        low_rank_state[:, :rank_count], adapter_up_weight[0], preferred_element_type=jnp.float32
    )
    value_rows = summed_output[:, half_split:column_width] + ADAPTER_SCALE * jnp.dot(
        low_rank_state[:, rank_count:], adapter_up_weight[1], preferred_element_type=jnp.float32
    )
    key_rows = rotate(key_rows.reshape(tok, KEY_VALUE_HEADS, HEAD_SIZE), token_positions).reshape(
        tok, half_split
    )
    own = jnp.concatenate([key_rows, value_rows], 1).astype(jnp.bfloat16)
    decode_cache = send_pages(own, page_lookup_table, groups)
    query_heads = queries[0].reshape(tok, KEY_VALUE_HEADS, group, HEAD_SIZE)
    scale = 1.0 / HEAD_SIZE**0.5
    tiles = tile_request_mask.shape[1]
    tile_ids = jnp.arange(tiles, dtype=jnp.int32)
    query_tile = token_positions // TILE
    query_onehot = (query_tile[:, None] == tile_ids[None, :]).astype(jnp.float32)
    live_rows = jnp.dot(query_onehot, tile_request_mask[0].astype(jnp.float32))
    length = lengths[0]
    initial = (
        jnp.full((KEY_VALUE_HEADS, group, tok, 1), -1e30, jnp.float32),
        jnp.zeros((KEY_VALUE_HEADS, group, tok, 1), jnp.float32),
        jnp.zeros((KEY_VALUE_HEADS, group, tok, HEAD_SIZE), jnp.float32),
    )
    state = initial
    piece = lax.all_gather(own, "ctx", axis=0, tiled=True)
    count = piece.shape[0]
    blk = 512
    blocks = piece.reshape(count // blk, blk, column_width)

    def inner(carry, item):
        offset, block = item
        peak, total, acc = carry
        kpos = offset * blk + jnp.arange(blk, dtype=jnp.int32)
        key_block = block[:, :half_split].reshape(blk, KEY_VALUE_HEADS, HEAD_SIZE)
        value_block = (
            block[:, half_split:].reshape(blk, KEY_VALUE_HEADS, HEAD_SIZE).astype(jnp.float32)
        )
        score = (
            jnp.einsum("qhgd,khd->hgqk", query_heads, key_block, preferred_element_type=jnp.float32)
            * scale
        )
        key_tile = kpos // TILE
        key_onehot = (key_tile[:, None] == tile_ids[None, :]).astype(jnp.float32)
        live = jnp.dot(live_rows, key_onehot.T) > 0.5
        live = live | (query_tile[:, None] == key_tile[None, :])
        allowed = (kpos[None, :] <= token_positions[:, None]) & (kpos[None, :] >= 0) & live & (
            kpos[None, :] < length
        ) | (kpos[None, :] == token_positions[:, None])
        masked = jnp.where(allowed, score, -1e30)
        new_peak = jnp.maximum(peak, jnp.max(masked, axis=-1, keepdims=True))
        expo = jnp.where(allowed, jnp.exp(masked - new_peak), 0.0)
        factor = jnp.exp(peak - new_peak)
        total = total * factor + jnp.sum(expo, axis=-1, keepdims=True)
        acc = acc * factor + jnp.einsum(
            "hgqk,khd->hgqd", expo, value_block, preferred_element_type=jnp.float32
        )
        return ((new_peak, total, acc), None)

    offsets = jnp.arange(count // blk, dtype=jnp.int32)
    state, _ = lax.scan(inner, state, (offsets, blocks))
    peak, total, acc = state
    out = acc / total
    out = jnp.transpose(out, (2, 0, 1, 3)).reshape(tok, HQ * HEAD_SIZE)
    out = jnp.where((token_positions < length)[:, None], out, 0.0)
    attended = out.astype(jnp.bfloat16)[None]
    return (attended, decode_cache)


def solution(mesh):
    in_specs = (
        P("grp", "ctx", None),
        P("grp", "ctx", None),
        P("grp", None),
        P("grp", None),
        P(),
        P("grp", None, None),
        P("grp"),
        P(None, "ctx"),
    )
    out_specs = (P("grp", "ctx", None), P("grp", "ctx", None, None))
    return jax.shard_map(local, mesh=mesh, in_specs=in_specs, out_specs=out_specs, check_vma=False)
```

profile of v0, /device:TPU:0, one launch (start us, length us, event | category | flops | bytes accessed | tf_op | source)
XLA Modules:
  0.0 115.5 jit_solution(12051520847819461086)
XLA Ops:
  7.2 0.0 copy-start
  7.2 1.9 %all_to_all.17 = bf16[64,4,2048]{2,1,0:T(4,128)(2,1)S(1)} reshape(bf16[1,64,8192]{2,1,0:T(8,128)(2,1)} %param.8) | data formatting | bytes 2097152 | tf_op jit(solution)/shard_map/all_to_all | solution.py:78
  9.1 1.5 %copy.31 = bf16[64,4,2048]{2,0,1:T(8,128)(2,1)} copy(bf16[64,4,2048]{2,1,0:T(4,128)(2,1)S(1)} %all_to_all.17) | data formatting | bytes 2097152 | tf_op jit(solution)/shard_map/all_to_all | solution.py:78
  10.6 4.2 %all-to-all-start = ((bf16[64,4,2048]{2,0,1:T(8,128)(2,1)}), bf16[64,4,2048]{2,0,1:T(8,128)(2,1)S(1)}, u32[]{:S(2)}, u32[]{:S(2)}) async-start(bf16[64,4,2048]{2,0,1:T(8,128)(2,1)} %copy.31), calls=%async_computation | async-start | bytes 2097152 | tf_op jit(solution)/shard_map/all_to_all | solution.py:78
  14.8 0.0 reduce-scatter.2.cloned.1.call-start
  14.9 14.4 %all-to-all-done = bf16[64,4,2048]{2,0,1:T(8,128)(2,1)S(1)} async-done(((bf16[64,4,2048]{2,0,1:T(8,128)(2,1)}), bf16[64,4,2048]{2,0,1:T(8,128)(2,1)S(1)}, u32[]{:S(2)}, u32[]{:S(2)}) %all-to-all-start) | async-done | bytes 1048608 | tf_op jit(solution)/shard_map/all_to_all | solution.py:78
  29.3 0.0 copy-done
  29.3 0.4 convolution_convert_fusion.2
  29.7 0.0 copy-start.3
  29.8 0.0 copy-start.2
  29.8 0.0 copy-start.1
  29.8 3.5 %convolution_convert_fusion.1 = bf16[256,1024]{1,0:T(8,128)(2,1)S(1)} fusion(bf16[256,2048]{1,0:T(8,128)(2,1)S(1)} %bitcast.71, bf16[2048,1024]{1,0:T(8,128)(2,1)} %param.10), kind=kOutput, calls=%fused_computation.15 | convolution fusion | flops 1074003968 | bytes 5767168 | tf_op jit(solution)/shard_map/dot_general | solution.py:82
  33.3 0.0 copy-start.4
  33.3 0.9 pad_maximum_fusion
  34.2 0.0 reduce-scatter.2.cloned.1.call-update
  34.2 0.0 all-gather.2.cloned.1.call-start
  34.9 0.0 copy-done.3
  35.0 0.2 convert_reduce_fusion
  35.2 0.2 multiply_cosine_fusion
  35.4 22.0 %reduce-scatter.2.cloned.1.call-done = bf16[64,1152]{1,0:T(8,128)(2,1)} async-done(((bf16[256,1152]{1,0:T(8,128)(2,1)}), bf16[64,1152]{1,0:T(8,128)(2,1)}) %reduce-scatter.2.cloned.1.call-update) | async-done | bytes 147472 | tf_op jit(solution)/shard_map/reduce_scatter | solution.py:79
  57.4 0.9 convert_element_type.53
  58.4 0.0 copy-done.2
  58.4 0.9 fusion.12
  59.3 0.2 multiply_subtract_fusion
  59.5 0.1 pad_maximum_fusion.1
  59.6 0.9 fusion.11
  60.5 0.7 maximum_convert_fusion
  61.2 0.0 all-gather.2.cloned.1.call-update
  61.2 0.0 copy-done.1
  61.2 0.1 copy.45
  61.4 0.4 and_reduce_fusion
  61.8 0.0 copy-done.4
  61.8 0.4 fusion.16
  62.2 1.0 reshape.298
  63.2 0.8 convolution_convert_fusion
  64.1 3.3 %all-to-all-start.1 = ((bf16[4,4,4096]{2,1,0:T(4,128)(2,1)}), bf16[4,4,4096]{2,1,0:T(4,128)(2,1)S(1)}, u32[]{:S(2)}, u32[]{:S(2)}) async-start(bf16[4,4,4096]{2,1,0:T(4,128)(2,1)} %convolution_convert_fusion), calls=%async_computation.2 | async-start | bytes 262144 | tf_op jit(solution)/shard_map/all_to_all | solution.py:45
  67.4 4.6 %all-to-all-done.1 = bf16[4,4,4096]{2,1,0:T(4,128)(2,1)S(1)} async-done(((bf16[4,4,4096]{2,1,0:T(4,128)(2,1)}), bf16[4,4,4096]{2,1,0:T(4,128)(2,1)S(1)}, u32[]{:S(2)}, u32[]{:S(2)}) %all-to-all-start.1) | async-done | bytes 131104 | tf_op jit(solution)/shard_map/all_to_all | solution.py:45
  72.0 0.2 fusion
  72.2 0.7 reshape.295
  73.0 28.6 %all-gather.2.cloned.1.call-done = bf16[512,1024]{1,0:T(8,128)(2,1)} async-done(((bf16[64,1024]{1,0:T(8,128)(2,1)}), bf16[512,1024]{1,0:T(8,128)(2,1)}) %all-gather.2.cloned.1.call-update) | async-done | bytes 1048592 | tf_op jit(solution)/shard_map/all_gather | solution.py:117
  101.6 1.3 %fusion.49 = (bf16[512,512]{1,0:T(8,128)(2,1)S(1)}, bf16[512,512]{1,0:T(8,128)(2,1)S(1)}) fusion(bf16[512,1024]{1,0:T(8,128)(2,1)} %all-gather.2.cloned.1.call-done), kind=kLoop, calls=%fused_computation.99 | loop fusion | bytes 2097152 | tf_op jit(solution)/shard_map/while/body/eval_jaxpr/slice | solution.py:128
  102.9 0.1 reshape.293
  103.0 0.1 reshape.292
  103.1 1.0 fusion.1
  104.2 1.3 %fusion.2 = f32[4,8,64]{2,1,0:T(8,128)S(1)} fusion(f32[4,512,64,8]{1,2,3,0:T(8,128)S(1)} %get-tuple-element.46, f32[4,8,64]{2,1,0:T(8,128)S(1)} %get-tuple-element.31, pred[64,512]{1,0:T(8,128)(4,1)S(1)} %fusion.16), kind=kLoop, calls=%fused_computation.6 | loop fusion | flops 5240832 | bytes 4243456 | tf_op jit(solution)/shard_map/while/body/eval_jaxpr/reduce_sum | solution.py:145
  105.5 1.6 %fusion.19 = bf16[64,4,8,128]{3,0,2,1:T(8,128)(2,1)S(1)} fusion(f32[4,512,64,8]{1,2,3,0:T(8,128)S(1)} %get-tuple-element.46, f32[4,8,64]{2,1,0:T(8,128)S(1)} %get-tuple-element.31, pred[64,512]{1,0:T(8,128)(4,1)S(1)} %fusion.16, bf16[512,4,128,1]{2,1,0,3:T(4,128)(2,1)S(1)} %bitcast.74, f32[64,4,8]{0,2,1:T(8,128)S(1)} %bitcast_add_fusion, ...), kind=kOutput, calls=%fused_computation.28 | convolution fusion | flops 273416192 | bytes 5300224 | tf_op jit(solution)/shard_map/while/body/eval_jaxpr/hgqk,khd->hgqd/dot_general | solution.py:146
  107.1 0.3 copy.36
  107.5 0.2 reshape.294
  107.7 1.0 select_convert_fusion
  (18 shorter events, 0.2 us)
Async XLA Ops:
  7.2 22.1 %copy-start = (bf16[2048,128]{1,0:T(8,128)(2,1)S(1)}, bf16[2048,128]{1,0:T(8,128)(2,1)}, u32[]{:S(2)}) copy-start(bf16[2048,128]{1,0:T(8,128)(2,1)} %param.11) | copy-start | bytes 1572868
  10.6 18.7 %all-to-all-start = ((bf16[64,4,2048]{2,0,1:T(8,128)(2,1)}), bf16[64,4,2048]{2,0,1:T(8,128)(2,1)S(1)}, u32[]{:S(2)}, u32[]{:S(2)}) async-start(bf16[64,4,2048]{2,0,1:T(8,128)(2,1)} %copy.31), calls=%async_computation | async-start | bytes 2097152 | tf_op jit(solution)/shard_map/all_to_all | solution.py:78
  14.8 42.6 %reduce-scatter.2.cloned.1.call-start = ((), (), s32[]{:S(2)}) async-start(), calls=%async_computation.3 | async-start | bytes 737280 | tf_op jit(solution)/shard_map/reduce_scatter | solution.py:79
  29.7 5.2 %copy-start.3 = (s32[4,16]{1,0:T(4,128)S(1)}, s32[4,16]{1,0:T(4,128)}, u32[]{:S(2)}) copy-start(s32[4,16]{1,0:T(4,128)} %param.15) | copy-start | bytes 772
  29.8 28.6 %copy-start.2 = (bf16[2,64,512]{2,1,0:T(8,128)(2,1)S(1)}, bf16[2,64,512]{2,1,0:T(8,128)(2,1)}, u32[]{:S(2)}) copy-start(bf16[2,64,512]{2,1,0:T(8,128)(2,1)} %param.12) | copy-start | bytes 393220
  29.8 31.5 %copy-start.1 = (bf16[1,64,4096]{2,1,0:T(8,128)(2,1)S(1)}, bf16[1,64,4096]{2,1,0:T(8,128)(2,1)}, u32[]{:S(2)}) copy-start(bf16[1,64,4096]{2,1,0:T(8,128)(2,1)} %param.9) | copy-start | bytes 1572868
  33.3 28.5 %copy-start.4 = (s32[1,4,4]{2,1,0:T(4,128)S(1)}, s32[1,4,4]{2,1,0:T(4,128)}, u32[]{:S(2)}) copy-start(s32[1,4,4]{2,1,0:T(4,128)} %param.13) | copy-start | bytes 196
  34.2 67.4 %all-gather.2.cloned.1.call-start = ((), (), s32[]{:S(2)}) async-start(), calls=%async_computation.4 | async-start | bytes 1179648 | tf_op jit(solution)/shard_map/all_gather | solution.py:117
  64.1 7.9 %all-to-all-start.1 = ((bf16[4,4,4096]{2,1,0:T(4,128)(2,1)}), bf16[4,4,4096]{2,1,0:T(4,128)(2,1)S(1)}, u32[]{:S(2)}, u32[]{:S(2)}) async-start(bf16[4,4,4096]{2,1,0:T(4,128)(2,1)} %convolution_convert_fusion), calls=%async_computation.2 | async-start | bytes 262144 | tf_op jit(solution)/shard_map/all_to_all | solution.py:45
Sparse Core Ops, SparseCore 0:
  34.3 23.0 reduce-scatter.1
  61.3 40.2 all-gather.1
where the time goes:
time: 116 us; the launch traced here: 115 us
  waiting for transfers between devices  69.7 us (60%)
  between operations  15 us (13%)
  matrix products  9.79 us (8%)
  starting transfers between devices  7.58 us (7%)
  local copies, waits for them, and re-layouts  7.46 us (6%)
  other arithmetic  5.95 us (5%)
    all_gather x1, waiting for transfers between devices, local(): piece = lax.all_gather(own, 'ctx', axis=0, tiled=True)  28.6 us
    reduce_scatter x1, waiting for transfers between devices, local(): lax.psum_scatter(jnp.concatenate([jnp.dot(mixed_output, key_value_weight,...  22 us
    all_to_all x1, waiting for transfers between devices, local(): lax.all_to_all(tokens[0], 'grp', split_axis=1, concat_axis=0, tiled=True)  14.4 us
    all_to_all x1, waiting for transfers between devices, send_pages(): lax.all_to_all(outgoing, 'grp', split_axis=0, concat_axis=0, tiled=True)  4.58 us
    all_to_all x1, starting transfers between devices, local(): lax.all_to_all(tokens[0], 'grp', split_axis=1, concat_axis=0, tiled=True)  4.21 us
    dot_general x1, matrix products, local(): jnp.dot(mixed_output, key_value_weight, preferred_element_type=jnp.float32)  3.5 us
    all_to_all x2, local copies, waits for them, and re-layouts, local(): lax.all_to_all(tokens[0], 'grp', split_axis=1, concat_axis=0, tiled=True)  3.45 us
    all_to_all x1, starting transfers between devices, send_pages(): lax.all_to_all(outgoing, 'grp', split_axis=0, concat_axis=0, tiled=True)  3.33 us
  transfers between devices with their start and end apart: 4, of which 4 were waited for; matrix products, arithmetic and copies ran while one was open for 4% of the time, Pallas kernels for 0%

commit v1 on v0

--- a/solution.py
+++ b/solution.py
@@ -114,7 +114,12 @@
         jnp.zeros((KEY_VALUE_HEADS, group, tok, HEAD_SIZE), jnp.float32),
     )
     state = initial
-    piece = lax.all_gather(own, "ctx", axis=0, tiled=True)
+    ring = [own]
+    for hop in range(7):
+        ring.append(lax.ppermute(ring[-1], "ctx", [(dev, (dev + 1) % 8) for dev in range(8)]))
+    piece = jnp.roll(
+        jnp.concatenate(ring[::-1], axis=0), (lax.axis_index("ctx") + 1) * ring[0].shape[0], axis=0
+    )
     count = piece.shape[0]
     blk = 512
     blocks = piece.reshape(count // blk, blk, column_width)

time: 116 us -> 128 us (1.10)
  waiting for transfers between devices: 69.7 us -> 83 us
  local copies, waits for them, and re-layouts: 7.46 us -> 5.55 us
  starting transfers between devices: 7.58 us -> 9.09 us
    ppermute x0 -> x7, waiting for transfers between devices: none -> 45.6 us  [local(): lax.ppermute(ring[-1], 'ctx', [(dev, (dev + 1) % 8) for dev in range(8)])]
    all_gather x1 -> x0, waiting for transfers between devices: 28.6 us -> none  [local(): piece = lax.all_gather(own, 'ctx', axis=0, tiled=True)]
    all_to_all x1, waiting for transfers between devices: 4.58 us -> 1.1 us  [send_pages(): lax.all_to_all(outgoing, 'grp', split_axis=0, concat_axis=0, tiled=True)]
    ppermute x0 -> x7, starting transfers between devices: none -> 1.56 us  [local(): lax.ppermute(ring[-1], 'ctx', [(dev, (dev + 1) % 8) for dev in range(8)])]
  transfers between devices with their start and end apart: 4 -> 10, of which waited for: 4 -> 10; matrix products, arithmetic and copies ran while one was open for 4% -> 3% of each run, Pallas kernels for 0% -> 0%
where the time goes in v1:
time: 128 us
  waiting for transfers between devices  83 us (65%)
  between operations  15.1 us (12%)
  matrix products  9.78 us (8%)
  starting transfers between devices  9.09 us (7%)
  local copies, waits for them, and re-layouts  5.55 us (4%)
  other arithmetic  5.32 us (4%)
    ppermute x7, waiting for transfers between devices, local(): lax.ppermute(ring[-1], 'ctx', [(dev, (dev + 1) % 8) for dev in range(8)])  45.6 us
    reduce_scatter x1, waiting for transfers between devices, local(): lax.psum_scatter(jnp.concatenate([jnp.dot(mixed_output, key_value_weight,...  22.5 us
    all_to_all x1, waiting for transfers between devices, local(): lax.all_to_all(tokens[0], 'grp', split_axis=1, concat_axis=0, tiled=True)  13.8 us
    all_to_all x1, starting transfers between devices, local(): lax.all_to_all(tokens[0], 'grp', split_axis=1, concat_axis=0, tiled=True)  4.21 us
    dot_general x1, matrix products, local(): jnp.dot(mixed_output, key_value_weight, preferred_element_type=jnp.float32)  3.48 us
    all_to_all x2, local copies, waits for them, and re-layouts, local(): lax.all_to_all(tokens[0], 'grp', split_axis=1, concat_axis=0, tiled=True)  3.46 us
    all_to_all x1, starting transfers between devices, send_pages(): lax.all_to_all(outgoing, 'grp', split_axis=0, concat_axis=0, tiled=True)  3.33 us
  transfers between devices with their start and end apart: 10, of which 10 were waited for; matrix products, arithmetic and copies ran while one was open for 3% of the time, Pallas kernels for 0%

profile of v1, /device:TPU:0, one launch (start us, length us, event | category | flops | bytes accessed | tf_op | source)
XLA Modules:
  0.0 127.9 jit_solution(12487116900666970511)
XLA Ops:
  7.2 0.0 copy-start
  7.2 1.9 %all_to_all.17 = bf16[64,4,2048]{2,1,0:T(4,128)(2,1)S(1)} reshape(bf16[1,64,8192]{2,1,0:T(8,128)(2,1)} %param.8) | data formatting | bytes 2097152 | tf_op jit(solution)/shard_map/all_to_all | solution.py:78
  9.1 1.6 %copy.31 = bf16[64,4,2048]{2,0,1:T(8,128)(2,1)} copy(bf16[64,4,2048]{2,1,0:T(4,128)(2,1)S(1)} %all_to_all.17) | data formatting | bytes 2097152 | tf_op jit(solution)/shard_map/all_to_all | solution.py:78
  10.6 4.2 %all-to-all-start = ((bf16[64,4,2048]{2,0,1:T(8,128)(2,1)}), bf16[64,4,2048]{2,0,1:T(8,128)(2,1)S(1)}, u32[]{:S(2)}, u32[]{:S(2)}) async-start(bf16[64,4,2048]{2,0,1:T(8,128)(2,1)} %copy.31), calls=%async_computation | async-start | bytes 2097152 | tf_op jit(solution)/shard_map/all_to_all | solution.py:78
  14.9 0.0 reduce-scatter.2.cloned.1.call-start
  15.5 13.8 %all-to-all-done = bf16[64,4,2048]{2,0,1:T(8,128)(2,1)S(1)} async-done(((bf16[64,4,2048]{2,0,1:T(8,128)(2,1)}), bf16[64,4,2048]{2,0,1:T(8,128)(2,1)S(1)}, u32[]{:S(2)}, u32[]{:S(2)}) %all-to-all-start) | async-done | bytes 1048608 | tf_op jit(solution)/shard_map/all_to_all | solution.py:78
  29.3 0.0 copy-done
  29.3 0.4 convolution_convert_fusion.2
  29.8 0.0 copy-start.3
  29.8 0.0 copy-start.4
  29.8 3.5 %convolution_convert_fusion.1 = bf16[256,1024]{1,0:T(8,128)(2,1)S(1)} fusion(bf16[256,2048]{1,0:T(8,128)(2,1)S(1)} %bitcast.71, bf16[2048,1024]{1,0:T(8,128)(2,1)} %param.10), kind=kOutput, calls=%fused_computation.15 | convolution fusion | flops 1074003968 | bytes 5767168 | tf_op jit(solution)/shard_map/dot_general | solution.py:82
  33.3 0.0 copy-start.2
  33.3 0.9 pad_maximum_fusion
  34.1 0.0 copy-start.1
  34.1 0.0 reduce-scatter.2.cloned.1.call-update
  34.2 0.0 copy-done.3
  34.3 0.0 copy-done.4
  34.3 0.4 fusion.16
  34.7 0.2 multiply_cosine_fusion
  34.9 22.5 %reduce-scatter.2.cloned.1.call-done = bf16[64,1152]{1,0:T(8,128)(2,1)} async-done(((bf16[256,1152]{1,0:T(8,128)(2,1)}), bf16[64,1152]{1,0:T(8,128)(2,1)}) %reduce-scatter.2.cloned.1.call-update) | async-done | bytes 147472 | tf_op jit(solution)/shard_map/reduce_scatter | solution.py:79
  57.4 0.9 convert_element_type.53
  58.4 0.0 copy-done.2
  58.4 0.9 fusion.12
  59.3 0.2 multiply_subtract_fusion
  59.5 0.1 pad_maximum_fusion.1
  59.6 0.9 fusion.11
  60.6 1.5 %collective-permute-start = (bf16[64,1024]{1,0:T(8,128)(2,1)S(1)}, bf16[64,1024]{1,0:T(8,128)(2,1)S(1)}, u32[]{:S(2)}, u32[]{:S(2)}) collective-permute-start(bf16[64,1024]{1,0:T(8,128)(2,1)S(1)} %maximum_convert_fusion), channel_id=1, source_target_pairs={{0,4},{4,8},{8,12},{12,16},{16,20},{20,24},{24,28},{28,0},{1,5},{5... | collective-permute-start | bytes 393224 | tf_op jit(solution)/shard_map/ppermute | solution.py:119
  62.1 6.4 %collective-permute-done = bf16[64,1024]{1,0:T(8,128)(2,1)S(1)} collective-permute-done((bf16[64,1024]{1,0:T(8,128)(2,1)S(1)}, bf16[64,1024]{1,0:T(8,128)(2,1)S(1)}, u32[]{:S(2)}, u32[]{:S(2)}) %collective-permute-start) | collective-permute-done | bytes 131104 | tf_op jit(solution)/shard_map/ppermute | solution.py:119
  68.5 0.0 collective-permute-start.1
  68.6 0.2 convert_reduce_fusion
  68.8 7.4 %collective-permute-done.1 = bf16[64,1024]{1,0:T(8,128)(2,1)S(1)} collective-permute-done((bf16[64,1024]{1,0:T(8,128)(2,1)S(1)}, bf16[64,1024]{1,0:T(8,128)(2,1)S(1)}, u32[]{:S(2)}, u32[]{:S(2)}) %collective-permute-start.1) | collective-permute-done | bytes 131104 | tf_op jit(solution)/shard_map/ppermute | solution.py:119
  76.2 0.0 collective-permute-start.2
  76.2 7.6 %collective-permute-done.2 = bf16[64,1024]{1,0:T(8,128)(2,1)S(1)} collective-permute-done((bf16[64,1024]{1,0:T(8,128)(2,1)S(1)}, bf16[64,1024]{1,0:T(8,128)(2,1)S(1)}, u32[]{:S(2)}, u32[]{:S(2)}) %collective-permute-start.2) | collective-permute-done | bytes 131104 | tf_op jit(solution)/shard_map/ppermute | solution.py:119
  83.9 0.0 collective-permute-start.3
  83.9 7.7 %collective-permute-done.3 = bf16[64,1024]{1,0:T(8,128)(2,1)S(1)} collective-permute-done((bf16[64,1024]{1,0:T(8,128)(2,1)S(1)}, bf16[64,1024]{1,0:T(8,128)(2,1)S(1)}, u32[]{:S(2)}, u32[]{:S(2)}) %collective-permute-start.3) | collective-permute-done | bytes 131104 | tf_op jit(solution)/shard_map/ppermute | solution.py:119
  91.5 0.0 collective-permute-start.4
  91.6 0.0 copy-done.1
  91.6 0.1 copy.45
  91.7 0.4 and_reduce_fusion
  92.0 0.1 reshape.298
  92.1 7.4 %collective-permute-done.4 = bf16[64,1024]{1,0:T(8,128)(2,1)S(1)} collective-permute-done((bf16[64,1024]{1,0:T(8,128)(2,1)S(1)}, bf16[64,1024]{1,0:T(8,128)(2,1)S(1)}, u32[]{:S(2)}, u32[]{:S(2)}) %collective-permute-start.4) | collective-permute-done | bytes 131104 | tf_op jit(solution)/shard_map/ppermute | solution.py:119
  99.5 0.0 collective-permute-start.5
  99.5 0.8 convolution_convert_fusion
  100.4 3.3 %all-to-all-start.1 = ((bf16[4,4,4096]{2,1,0:T(4,128)(2,1)}), bf16[4,4,4096]{2,1,0:T(4,128)(2,1)S(1)}, u32[]{:S(2)}, u32[]{:S(2)}) async-start(bf16[4,4,4096]{2,1,0:T(4,128)(2,1)} %convolution_convert_fusion), calls=%async_computation.2 | async-start | bytes 262144 | tf_op jit(solution)/shard_map/all_to_all | solution.py:45
  103.7 3.5 %collective-permute-done.5 = bf16[64,1024]{1,0:T(8,128)(2,1)S(1)} collective-permute-done((bf16[64,1024]{1,0:T(8,128)(2,1)S(1)}, bf16[64,1024]{1,0:T(8,128)(2,1)S(1)}, u32[]{:S(2)}, u32[]{:S(2)}) %collective-permute-start.5) | collective-permute-done | bytes 131104 | tf_op jit(solution)/shard_map/ppermute | solution.py:119
  107.2 0.0 collective-permute-start.6
  107.2 1.1 all-to-all-done.1
  108.3 0.2 fusion
  108.6 0.7 reshape.295
  109.3 5.6 %collective-permute-done.6 = bf16[64,1024]{1,0:T(8,128)(2,1)S(1)} collective-permute-done((bf16[64,1024]{1,0:T(8,128)(2,1)S(1)}, bf16[64,1024]{1,0:T(8,128)(2,1)S(1)}, u32[]{:S(2)}, u32[]{:S(2)}) %collective-permute-start.6) | collective-permute-done | bytes 131104 | tf_op jit(solution)/shard_map/ppermute | solution.py:119
  115.2 0.1 fusion.51
  115.3 0.1 reshape.293
  115.4 0.1 reshape.292
  115.6 1.0 fusion.1
  116.6 1.3 %fusion.2 = f32[4,8,64]{2,1,0:T(8,128)S(1)} fusion(f32[4,512,64,8]{1,2,3,0:T(8,128)S(1)} %get-tuple-element.46, f32[4,8,64]{2,1,0:T(8,128)S(1)} %get-tuple-element.31, pred[64,512]{1,0:T(8,128)(4,1)S(1)} %fusion.16), kind=kLoop, calls=%fused_computation.6 | loop fusion | flops 5240832 | bytes 4243456 | tf_op jit(solution)/shard_map/while/body/eval_jaxpr/reduce_sum | solution.py:150
  118.0 1.6 %fusion.19 = bf16[64,4,8,128]{3,0,2,1:T(8,128)(2,1)S(1)} fusion(f32[4,512,64,8]{1,2,3,0:T(8,128)S(1)} %get-tuple-element.46, f32[4,8,64]{2,1,0:T(8,128)S(1)} %get-tuple-element.31, pred[64,512]{1,0:T(8,128)(4,1)S(1)} %fusion.16, bf16[512,4,128,1]{2,1,0,3:T(4,128)(2,1)S(1)} %bitcast.77, f32[64,4,8]{0,2,1:T(8,128)S(1)} %bitcast_add_fusion, ...), kind=kOutput, calls=%fused_computation.28 | convolution fusion | flops 273416192 | bytes 5300224 | tf_op jit(solution)/shard_map/while/body/eval_jaxpr/hgqk,khd->hgqd/dot_general | solution.py:151
  119.5 0.3 copy.36
  119.9 0.2 reshape.294
  120.1 1.0 select_convert_fusion
  (35 shorter events, 0.4 us)
Async XLA Ops:
  7.2 22.2 %copy-start = (bf16[2048,128]{1,0:T(8,128)(2,1)S(1)}, bf16[2048,128]{1,0:T(8,128)(2,1)}, u32[]{:S(2)}) copy-start(bf16[2048,128]{1,0:T(8,128)(2,1)} %param.11) | copy-start | bytes 1572868
  10.6 18.7 %all-to-all-start = ((bf16[64,4,2048]{2,0,1:T(8,128)(2,1)}), bf16[64,4,2048]{2,0,1:T(8,128)(2,1)S(1)}, u32[]{:S(2)}, u32[]{:S(2)}) async-start(bf16[64,4,2048]{2,0,1:T(8,128)(2,1)} %copy.31), calls=%async_computation | async-start | bytes 2097152 | tf_op jit(solution)/shard_map/all_to_all | solution.py:78
  14.9 42.6 %reduce-scatter.2.cloned.1.call-start = ((), (), s32[]{:S(2)}) async-start(), calls=%async_computation.3 | async-start | bytes 737280 | tf_op jit(solution)/shard_map/reduce_scatter | solution.py:79
  29.8 4.5 %copy-start.3 = (s32[4,16]{1,0:T(4,128)S(1)}, s32[4,16]{1,0:T(4,128)}, u32[]{:S(2)}) copy-start(s32[4,16]{1,0:T(4,128)} %param.15) | copy-start | bytes 772
  29.8 4.5 %copy-start.4 = (s32[1,4,4]{2,1,0:T(4,128)S(1)}, s32[1,4,4]{2,1,0:T(4,128)}, u32[]{:S(2)}) copy-start(s32[1,4,4]{2,1,0:T(4,128)} %param.13) | copy-start | bytes 196
  33.3 25.1 %copy-start.2 = (bf16[2,64,512]{2,1,0:T(8,128)(2,1)S(1)}, bf16[2,64,512]{2,1,0:T(8,128)(2,1)}, u32[]{:S(2)}) copy-start(bf16[2,64,512]{2,1,0:T(8,128)(2,1)} %param.12) | copy-start | bytes 393220
  34.1 57.4 %copy-start.1 = (bf16[1,64,4096]{2,1,0:T(8,128)(2,1)S(1)}, bf16[1,64,4096]{2,1,0:T(8,128)(2,1)}, u32[]{:S(2)}) copy-start(bf16[1,64,4096]{2,1,0:T(8,128)(2,1)} %param.9) | copy-start | bytes 1572868
  60.6 8.0 %collective-permute-start = (bf16[64,1024]{1,0:T(8,128)(2,1)S(1)}, bf16[64,1024]{1,0:T(8,128)(2,1)S(1)}, u32[]{:S(2)}, u32[]{:S(2)}) collective-permute-start(bf16[64,1024]{1,0:T(8,128)(2,1)S(1)} %maximum_convert_fusion), channel_id=1, source_target_pairs={{0,4},{4,8},{8,12},{12,16},{16,20},{20,24},{24,28},{28,0},{1,5},{5... | collective-permute-start | bytes 393224 | tf_op jit(solution)/shard_map/ppermute | solution.py:119
  68.5 7.7 %collective-permute-start.1 = (bf16[64,1024]{1,0:T(8,128)(2,1)S(1)}, bf16[64,1024]{1,0:T(8,128)(2,1)S(1)}, u32[]{:S(2)}, u32[]{:S(2)}) collective-permute-start(bf16[64,1024]{1,0:T(8,128)(2,1)S(1)} %collective-permute-done), channel_id=1, source_target_pairs={{0,4},{4,8},{8,12},{12,16},{16,20},{20,24},{24,28},{28,0},{1,5},{5... | collective-permute-start | bytes 393224 | tf_op jit(solution)/shard_map/ppermute | solution.py:119
  76.2 7.7 %collective-permute-start.2 = (bf16[64,1024]{1,0:T(8,128)(2,1)S(1)}, bf16[64,1024]{1,0:T(8,128)(2,1)S(1)}, u32[]{:S(2)}, u32[]{:S(2)}) collective-permute-start(bf16[64,1024]{1,0:T(8,128)(2,1)S(1)} %collective-permute-done.1), channel_id=1, source_target_pairs={{0,4},{4,8},{8,12},{12,16},{16,20},{20,24},{24,28},{28,0},{1,5},{5... | collective-permute-start | bytes 393224 | tf_op jit(solution)/shard_map/ppermute | solution.py:119
  83.9 7.7 %collective-permute-start.3 = (bf16[64,1024]{1,0:T(8,128)(2,1)S(1)}, bf16[64,1024]{1,0:T(8,128)(2,1)S(1)}, u32[]{:S(2)}, u32[]{:S(2)}) collective-permute-start(bf16[64,1024]{1,0:T(8,128)(2,1)S(1)} %collective-permute-done.2), channel_id=1, source_target_pairs={{0,4},{4,8},{8,12},{12,16},{16,20},{20,24},{24,28},{28,0},{1,5},{5... | collective-permute-start | bytes 393224 | tf_op jit(solution)/shard_map/ppermute | solution.py:119
  91.5 8.0 %collective-permute-start.4 = (bf16[64,1024]{1,0:T(8,128)(2,1)S(1)}, bf16[64,1024]{1,0:T(8,128)(2,1)S(1)}, u32[]{:S(2)}, u32[]{:S(2)}) collective-permute-start(bf16[64,1024]{1,0:T(8,128)(2,1)S(1)} %collective-permute-done.3), channel_id=1, source_target_pairs={{0,4},{4,8},{8,12},{12,16},{16,20},{20,24},{24,28},{28,0},{1,5},{5... | collective-permute-start | bytes 393224 | tf_op jit(solution)/shard_map/ppermute | solution.py:119
  99.5 7.7 %collective-permute-start.5 = (bf16[64,1024]{1,0:T(8,128)(2,1)S(1)}, bf16[64,1024]{1,0:T(8,128)(2,1)S(1)}, u32[]{:S(2)}, u32[]{:S(2)}) collective-permute-start(bf16[64,1024]{1,0:T(8,128)(2,1)S(1)} %collective-permute-done.4), channel_id=1, source_target_pairs={{0,4},{4,8},{8,12},{12,16},{16,20},{20,24},{24,28},{28,0},{1,5},{5... | collective-permute-start | bytes 393224 | tf_op jit(solution)/shard_map/ppermute | solution.py:119
  100.4 7.9 %all-to-all-start.1 = ((bf16[4,4,4096]{2,1,0:T(4,128)(2,1)}), bf16[4,4,4096]{2,1,0:T(4,128)(2,1)S(1)}, u32[]{:S(2)}, u32[]{:S(2)}) async-start(bf16[4,4,4096]{2,1,0:T(4,128)(2,1)} %convolution_convert_fusion), calls=%async_computation.2 | async-start | bytes 262144 | tf_op jit(solution)/shard_map/all_to_all | solution.py:45
  107.2 7.7 %collective-permute-start.6 = (bf16[64,1024]{1,0:T(8,128)(2,1)S(1)}, bf16[64,1024]{1,0:T(8,128)(2,1)S(1)}, u32[]{:S(2)}, u32[]{:S(2)}) collective-permute-start(bf16[64,1024]{1,0:T(8,128)(2,1)S(1)} %collective-permute-done.5), channel_id=1, source_target_pairs={{0,4},{4,8},{8,12},{12,16},{16,20},{20,24},{24,28},{28,0},{1,5},{5... | collective-permute-start | bytes 393224 | tf_op jit(solution)/shard_map/ppermute | solution.py:119
Sparse Core Ops, SparseCore 0:
  34.3 23.0 reduce-scatter.1
